TPU v7x, 256 devices: a whole 4x4x8 slice. The times are simulated.
256 devices in a mesh: lat: 16 (over y_lo, x, core), lon: 16 (over y_hi, z).
Axes of the slice: x: 4, y: 4 (y_hi: 2, y_lo: 2; y = y_hi * 2 + y_lo), z: 8, core: 2. Of those that a mesh axis runs over, the one named last changes fastest.
Arguments:
- fields: bfloat16 [32, 128, 4096], P(None, 'lat', 'lon'), may hold values from -6 to 6
- cotangent: bfloat16 [32, 128, 4096], P(None, 'lat', 'lon'), may hold values from -0.008239746 to 0.008239746
- kernel_in: bfloat16 [9, 128, 32], replicated, may hold values from -0.375 to 0.375
- kernel_mid: bfloat16 [9, 128, 128], replicated, may hold values from -0.1875 to 0.1875
- kernel_out: bfloat16 [9, 32, 128], replicated, may hold values from -0.1875 to 0.1875
- patch_anchors: int32 [16, 16, 4, 2], P('lat', 'lon'), may hold values from 0 to 8
- blend_weights: int32 [4, 128, 4096], P(None, 'lat', 'lon'), may hold values from 1 to 8
- tile_counts: int32 [16, 16], P('lat', 'lon'), may hold values from 0 to 4, as said below
Outputs:
- blended: float32 [32, 128, 4096], P(None, 'lat', 'lon')
- grad_in: float32 [9, 128, 32], replicated
- grad_mid: float32 [9, 128, 128], replicated
- grad_out: float32 [9, 32, 128], replicated
Inputs may be any that keep to these rules, and one draw needn't show every extreme that they name: `tile_counts`: the counts of the tiles in lat rows i and i + 8 at the same lon sum to exactly 4; tile (1, 0) holds 4 patches and tile (9, 0) none.
All inputs are finite; a program needn't handle non-finite values.
Results may differ from a plain program's by a relative error of at most 0.005.
Values may be sent and summed in bfloat16 or wider, within the bound.
A program may use at most 64 MiB of HBM per device.

v0:
```python
import jax
import jax.numpy as jnp
from jax import lax
from jax.sharding import PartitionSpec as P

MARGIN = 4
SLOTS = 4
KERNEL_TAPS = ((0, 0), (0, 1), (0, 2), (1, 0), (1, 1), (1, 2), (2, 0), (2, 1), (2, 2))


def extended_2(block, sides, width):
    for axis, dim in sides:
        count = lax.axis_size(axis)
        forward = [(i, i + 1) for i in range(count - 1)]
        forward.append((count - 1, 0))
        backward = [(target, source) for source, target in forward]
        low = lax.ppermute(
            lax.slice_in_dim(block, block.shape[dim] - width, None, axis=dim), axis, forward
        )
        high = lax.ppermute(lax.slice_in_dim(block, 0, width, axis=dim), axis, backward)
        block = jnp.concatenate([low, block, high], axis=dim)
    return block


def shifted(value, axis, steps):
    count = lax.axis_size(axis)
    pairs = [(source, (source + steps) % count) for source in range(count)]
    return lax.ppermute(value, axis, pairs)


def forward_conv(values, kernel):
    height, breadth = (values.shape[1], values.shape[2])
    padded = jnp.pad(values, ((0, 0), (1, 1), (1, 1)))
    summed = jnp.zeros((kernel.shape[1], height, breadth), jnp.float32)
    for tap_index, (tap_row, tap_col) in enumerate(KERNEL_TAPS):
        summed = summed + jnp.einsum(
            "ok,khw->ohw",
            kernel[tap_index],
            padded[:, tap_row : tap_row + height, tap_col : tap_col + breadth],
            preferred_element_type=jnp.float32,
        )
    return summed


def backward_conv(cotangent, kernel):
    height, breadth = (cotangent.shape[1], cotangent.shape[2])
    padded = jnp.pad(cotangent, ((0, 0), (1, 1), (1, 1)))
    summed = jnp.zeros((kernel.shape[2], height, breadth), jnp.float32)
    for tap_index, (tap_row, tap_col) in enumerate(KERNEL_TAPS):
        summed = summed + jnp.einsum(
            "ok,ohw->khw",
            kernel[tap_index],
            padded[:, 2 - tap_row : 2 - tap_row + height, 2 - tap_col : 2 - tap_col + breadth],
            preferred_element_type=jnp.float32,
        )
    return summed


def kernel_grad(cotangent, values):
    height, breadth = (values.shape[1], values.shape[2])
    padded = jnp.pad(values, ((0, 0), (1, 1), (1, 1)))
    pieces = [
        jnp.einsum(
            "ohw,khw->ok",
            cotangent,
            padded[:, tap_row : tap_row + height, tap_col : tap_col + breadth],
            preferred_element_type=jnp.float32,
        )
        for tap_row, tap_col in KERNEL_TAPS
    ]
    return jnp.stack(pieces)


def silu_slope(pre_act):
    sigmoid = jax.nn.sigmoid(pre_act)
    return sigmoid * (1.0 + pre_act * (1.0 - sigmoid))


def patch_pass(inputs, out_grad, kernel_in, kernel_mid, kernel_out):
    pre_one = forward_conv(inputs, kernel_in)
    hidden_one = jax.nn.silu(pre_one).astype(jnp.bfloat16)
    pre_two = forward_conv(hidden_one, kernel_mid)
    hidden_two = (hidden_one.astype(jnp.float32) + jax.nn.silu(pre_two)).astype(jnp.bfloat16)
    result = forward_conv(hidden_two, kernel_out)
    grad_two = backward_conv(out_grad, kernel_out)
    delta_two = (grad_two * silu_slope(pre_two)).astype(jnp.bfloat16)
    grad_one = grad_two + backward_conv(delta_two, kernel_mid)
    delta_one = (grad_one * silu_slope(pre_one)).astype(jnp.bfloat16)
    return (
        result,
        kernel_grad(delta_one, inputs),
        kernel_grad(delta_two, hidden_one),
        kernel_grad(out_grad, hidden_two),
    )


def run_patches(inputs, out_grads, kernel_in, kernel_mid, kernel_out):
    initial = (
        jnp.zeros(kernel_in.shape, jnp.float32),
        jnp.zeros(kernel_mid.shape, jnp.float32),
        jnp.zeros(kernel_out.shape, jnp.float32),
    )

    def step_patch(running, slot_pair):
        result, part_in, part_mid, part_out = patch_pass(
            slot_pair[0], slot_pair[1], kernel_in, kernel_mid, kernel_out
        )
        return ((running[0] + part_in, running[1] + part_mid, running[2] + part_out), result)

    return lax.scan(step_patch, initial, (inputs, out_grads))


def fold_canvas(canvas, keep_top, keep_bottom):
    extended = extended_2(canvas, (("lat", 1), ("lon", 2)), MARGIN)
    height = canvas.shape[1] - 2 * MARGIN
    breadth = canvas.shape[2] - 2 * MARGIN
    inner_rows = slice(2 * MARGIN, 2 * MARGIN + height)
    inner_cols = slice(2 * MARGIN, 2 * MARGIN + breadth)
    center_part = extended[:, inner_rows, inner_cols]
    col_left = ((0, 0), (0, 0), (0, breadth - MARGIN))
    col_right = ((0, 0), (0, 0), (breadth - MARGIN, 0))
    upper_part = (
        extended[:, :MARGIN, inner_cols]
        + jnp.pad(extended[:, :MARGIN, :MARGIN], col_left)
        + jnp.pad(extended[:, :MARGIN, -MARGIN:], col_right)
    )
    lower_part = (
        extended[:, -MARGIN:, inner_cols]
        + jnp.pad(extended[:, -MARGIN:, :MARGIN], col_left)
        + jnp.pad(extended[:, -MARGIN:, -MARGIN:], col_right)
    )
    summed = (
        center_part
        + jnp.pad(extended[:, inner_rows, :MARGIN], col_left)
        + jnp.pad(extended[:, inner_rows, -MARGIN:], col_right)
    )
    summed = summed + jnp.pad(upper_part * keep_top, ((0, 0), (0, height - MARGIN), (0, 0)))
    summed = summed + jnp.pad(lower_part * keep_bottom, ((0, 0), (height - MARGIN, 0), (0, 0)))
    return summed


def shards(
    fields, cotangent, kernel_in, kernel_mid, kernel_out, patch_anchors, blend_weights, tile_counts
):
    channels, height, breadth = (fields.shape[0], fields.shape[1], fields.shape[2])
    canvas_rows = height + 2 * MARGIN
    canvas_cols = breadth + 2 * MARGIN
    lat_size = lax.axis_size("lat")
    lat_index = lax.axis_index("lat")
    keep_top = (lat_index > 0).astype(jnp.float32)
    keep_bottom = (lat_index < lat_size - 1).astype(jnp.float32)
    slot_count = tile_counts[0, 0]
    slot_live = (jnp.arange(SLOTS) < slot_count).astype(jnp.int32)
    weights = (blend_weights * slot_live[:, None, None]).astype(jnp.float32)
    starts = patch_anchors[0, 0]

    def place_slots(per_slot):
        canvas = jnp.zeros((per_slot.shape[1], canvas_rows, canvas_cols), jnp.float32)
        for slot_index in range(SLOTS):
            corner = (jnp.int32(0), starts[slot_index, 0], starts[slot_index, 1])
            current = lax.dynamic_slice(canvas, corner, per_slot.shape[1:])
            canvas = lax.dynamic_update_slice(canvas, current + per_slot[slot_index], corner)
        return canvas

    total_weight = jnp.maximum(
        fold_canvas(place_slots(weights[:, None]), keep_top, keep_bottom), 1.0
    )
    scaled = (cotangent.astype(jnp.float32) / total_weight).astype(jnp.bfloat16)
    wide_fields, wide_scaled = (
        extended_2(fields, (("lat", 1), ("lon", 2)), MARGIN),
        extended_2(scaled, (("lat", 1), ("lon", 2)), MARGIN),
    )
    row_ids = jnp.arange(canvas_rows)[None, :, None]
    keep_rows = ((row_ids >= MARGIN) | (keep_top > 0.0)) & (
        (row_ids < height + MARGIN) | (keep_bottom > 0.0)
    )
    wide_fields = jnp.where(keep_rows, wide_fields, jnp.zeros_like(wide_fields))
    wide_scaled = jnp.where(keep_rows, wide_scaled, jnp.zeros_like(wide_scaled))
    window_list = []
    grad_list = []
    for slot_index in range(SLOTS):
        corner = (jnp.int32(0), starts[slot_index, 0], starts[slot_index, 1])
        window_list.append(lax.dynamic_slice(wide_fields, corner, (channels, height, breadth)))
        scaled_window = lax.dynamic_slice(wide_scaled, corner, (channels, height, breadth)).astype(
            jnp.float32
        )
        grad_list.append((weights[slot_index] * scaled_window).astype(jnp.bfloat16))
    inputs = jnp.stack(window_list)
    out_grads = jnp.stack(grad_list)
    half_slots = SLOTS // 2
    upper_half = (lat_index >= lat_size // 2).astype(jnp.int32)
    first_count = jnp.where(upper_half == 0, slot_count, SLOTS - slot_count)
    outgoing_inputs = jnp.where(upper_half == 0, inputs[half_slots:], inputs[:half_slots])
    outgoing_grads = jnp.where(upper_half == 0, out_grads[half_slots:], out_grads[:half_slots])
    incoming_inputs, incoming_grads = shifted(
        (outgoing_inputs, outgoing_grads), "lat", lat_size // 2
    )
    table_inputs = jnp.concatenate([inputs, incoming_inputs], axis=0)
    table_grads = jnp.concatenate([out_grads, incoming_grads], axis=0)
    position = upper_half * half_slots + jnp.arange(half_slots, dtype=jnp.int32)
    picked = jnp.where(
        position < first_count,
        jnp.where(upper_half == 0, position, position + SLOTS - half_slots),
        jnp.where(upper_half == 0, SLOTS + position - first_count, position - first_count),
    )
    picked = jnp.clip(picked, 0, SLOTS + half_slots - 1)
    totals, computed = run_patches(
        jnp.take(table_inputs, picked, axis=0),
        jnp.take(table_grads, picked, axis=0),
        kernel_in,
        kernel_mid,
        kernel_out,
    )
    returned = shifted(computed, "lat", lat_size // 2)
    ordered = jnp.where(
        upper_half == 0,
        jnp.concatenate([computed, returned], axis=0),
        jnp.concatenate([returned, computed], axis=0),
    )
    where_slot = jnp.clip(
        jnp.arange(SLOTS, dtype=jnp.int32) + upper_half * first_count, 0, SLOTS - 1
    )
    outputs = jnp.take(ordered, where_slot, axis=0)
    weighted = weights[:, None] * outputs
    numerator = fold_canvas(place_slots(weighted), keep_top, keep_bottom)
    blended = numerator / total_weight
    summed_grads = lax.psum((totals[0], totals[1], totals[2]), ("lat", "lon"))
    return (blended, summed_grads[0], summed_grads[1], summed_grads[2])


def solution(mesh):
    return jax.shard_map(
        shards,
        mesh=mesh,
        in_specs=(
            P(None, "lat", "lon"),
            P(None, "lat", "lon"),
            P(),
            P(),
            P(),
            P("lat", "lon", None, None),
            P(None, "lat", "lon"),
            P("lat", "lon"),
        ),
        out_specs=(P(None, "lat", "lon"), P(), P(), P()),
        check_vma=False,
    )
```

profile of v0, /device:TPU:1, one launch (start us, length us, event | category | flops | bytes accessed | tf_op | source)
XLA Modules:
  0.0 498.2 jit_solution(12220531734381858021)
XLA Ops:
  27.7 2.6 collective-permute-start
  31.2 3.8 collective-permute-start.10
  35.4 7.0 %collective-permute-start.3 = (f32[1,24,4]{2,1,0:T(8,128)S(1)}, f32[1,24,4]{2,1,0:T(8,128)S(1)}, u32[]{:S(2)}, u32[]{:S(2)}) collective-permute-start(f32[1,24,4]{2,1,0:T(8,128)S(1)} %get-tuple-element.254), channel_id=1, source_target_pairs={{1,0},{2,1},{3,2},{4,3},{5,4},{6,5},{7,6},{8,7},{9,8},{10,9},{11,1... | collective-permute-start | bytes 1160 | tf_op jit(solution)/shard_map/ppermute | solution.py:20
  42.4 1.0 collective-permute-done.2
  46.1 5.5 %collective-permute-start.12 = (bf16[32,16,4]{2,1,0:T(8,128)(2,1)S(1)}, bf16[32,16,4]{2,1,0:T(8,128)(2,1)S(1)}, u32[]{:S(2)}, u32[]{:S(2)}) collective-permute-start(bf16[32,16,4]{2,1,0:T(8,128)(2,1)S(1)} %get-tuple-element.246), channel_id=1, source_target_pairs={{1,0},{2,1},{3,2},{4,3},{5,4},{6,5},{7,6},{8,7},{9,8},{10,9},{11,1... | collective-permute-start | bytes 12296 | tf_op jit(solution)/shard_map/ppermute | solution.py:20
  52.0 18.8 %collective-permute-start.7 = (bf16[32,16,4]{2,1,0:T(8,128)(2,1)S(1)}, bf16[32,16,4]{2,1,0:T(8,128)(2,1)S(1)}, u32[]{:S(2)}, u32[]{:S(2)}) collective-permute-start(bf16[32,16,4]{2,1,0:T(8,128)(2,1)S(1)} %get-tuple-element.248), channel_id=1, source_target_pairs={{1,0},{2,1},{3,2},{4,3},{5,4},{6,5},{7,6},{8,7},{9,8},{10,9},{11,1... | collective-permute-start | bytes 12296 | tf_op jit(solution)/shard_map/ppermute | solution.py:20
  70.8 1.9 collective-permute-done.7
  72.7 1.0 maximum_select_fusion.2
  76.7 3.1 collective-permute-done.8
  80.4 2.2 collective-permute-done.13
  84.2 72.5 %while.19 = (s32[]{:T(128)}, f32[9,128,32]{1,2,0:T(8,128)S(1)}, f32[9,128,128]{2,1,0:T(8,128)S(1)}, f32[9,32,128]{2,1,0:T(8,128)}, f32[2,32,8,256]{3,2,1,0:T(8,1...) while((s32[]{:T(128)}, f32[9,128,32]{1,2,0:T(8,128)S(1)}, ...), condition=%wide.region_1.3_spmd.clone, body=%wide.region_0.2_spmd.clone.sunk | while | flops 2583609344 | bytes 133587216 | solution.py:110
  84.2 1.0 constant_dynamic-slice_fusion.3
  88.7 1.6 multiply_convert_fusion.8
  108.5 1.6 select_add_fusion.8
  115.7 0.9 copy-done.20
  120.4 1.0 constant_dynamic-slice_fusion.3
  124.9 1.6 multiply_convert_fusion.8
  144.7 1.7 select_add_fusion.8
  157.5 7.5 %collective-permute-done.14 = f32[2,32,8,256]{3,2,1,0:T(8,128)S(1)} collective-permute-done((f32[2,32,8,256]{3,2,1,0:T(8,128)}, f32[2,32,8,256]{3,2,1,0:T(8,128)S(1)}, u32[]{:S(2)}, u32[]{:S(2)}) %collective-permute-start.14) | collective-permute-done | bytes 524320 | tf_op jit(solution)/shard_map/ppermute | solution.py:28
  165.0 1.3 maximum_select_fusion
  167.3 10.2 %dynamic_update_slice.35 = f32[32,16,264]{2,1,0:T(8,128)S(1)} dynamic-update-slice(f32[32,16,264]{2,1,0:T(8,128)S(1)} %broadcast_in_dim.59, f32[32,8,256]{2,1,0:T(8,128)S(1)} %slice_bitcast_fusion.3, s32[]{:T(128)} %constant.84.clone.1, s32[]{:T(128)S(6)} %select_n.136, s32[]{:T(128)S(6)} %select_n.137) | dynamic-update-slice | bytes 524292 | tf_op jit(solution)/shard_map/dynamic_update_slice | solution.py:162
  177.6 10.2 %dynamic_update_slice.36 = f32[32,16,264]{2,1,0:T(8,128)S(1)} dynamic-update-slice(f32[32,16,264]{2,1,0:T(8,128)S(1)} %dynamic_update_slice.35, f32[32,8,256]{2,1,0:T(8,128)S(1)} %fusion.200, s32[]{:T(128)} %constant.84.clone.1, s32[]{:T(128)S(6)} %select_n.138, s32[]{:T(128)S(6)} %select_n.139) | dynamic-update-slice | bytes 524292 | tf_op jit(solution)/shard_map/dynamic_update_slice | solution.py:162
  188.0 1.3 dynamic_update_slice.37
  189.4 10.2 %dynamic_update_slice.38 = f32[32,16,264]{2,1,0:T(8,128)S(1)} dynamic-update-slice(f32[32,16,264]{2,1,0:T(8,128)S(1)} %dynamic_update_slice.37, f32[32,8,256]{2,1,0:T(8,128)S(1)} %fusion.198, s32[]{:T(128)} %constant.84.clone.1, s32[]{:T(128)S(6)} %select_n.142, s32[]{:T(128)S(6)} %select_n.143) | dynamic-update-slice | bytes 524292 | tf_op jit(solution)/shard_map/dynamic_update_slice | solution.py:162
  199.6 9.2 %collective-permute-start.15 = (f32[32,4,264]{2,1,0:T(4,128)S(1)}, f32[32,4,264]{2,1,0:T(4,128)S(1)}, u32[]{:S(2)}, u32[]{:S(2)}) collective-permute-start(f32[32,4,264]{2,1,0:T(4,128)S(1)} %get-tuple-element.239), channel_id=1, source_target_pairs={{0,16},{16,32},{32,48},{48,64},{64,80},{80,96},{96,112},{112,128},... | collective-permute-start | bytes 405512 | tf_op jit(solution)/shard_map/ppermute | solution.py:17
  208.8 2.6 collective-permute-done.15
  211.4 6.6 %collective-permute-done.16 = f32[32,4,264]{2,1,0:T(4,128)S(1)} collective-permute-done((f32[32,4,264]{2,1,0:T(4,128)S(1)}, f32[32,4,264]{2,1,0:T(4,128)S(1)}, u32[]{:S(2)}, u32[]{:S(2)}) %collective-permute-start.16) | collective-permute-done | bytes 135200 | tf_op jit(solution)/shard_map/ppermute | solution.py:20
  218.4 11.1 %collective-permute-start.18 = (f32[32,24,4]{2,1,0:T(8,128)S(1)}, f32[32,24,4]{2,1,0:T(8,128)S(1)}, u32[]{:S(2)}, u32[]{:S(2)}) collective-permute-start(f32[32,24,4]{2,1,0:T(8,128)S(1)} %get-tuple-element.238), channel_id=1, source_target_pairs={{1,0},{2,1},{3,2},{4,3},{5,4},{6,5},{7,6},{8,7},{9,8},{10,9},{11,1... | collective-permute-start | bytes 36872 | tf_op jit(solution)/shard_map/ppermute | solution.py:20
  229.4 5.5 %collective-permute-done.17 = f32[32,24,4]{2,1,0:T(8,128)S(1)} collective-permute-done((f32[32,24,4]{2,1,0:T(8,128)S(1)}, f32[32,24,4]{2,1,0:T(8,128)S(1)}, u32[]{:S(2)}, u32[]{:S(2)}) %collective-permute-start.17) | collective-permute-done | bytes 12320 | tf_op jit(solution)/shard_map/ppermute | solution.py:17
  238.5 248.2 %all-reduce.24.cloned.1.call-done = (f32[9,128,32]{1,2,0:T(8,128)}, f32[9,128,128]{2,1,0:T(8,128)}, f32[9,32,128]{2,1,0:T(8,128)}) async-done(((f32[9,128,32]{1,2,0:T(8,128)}, f32[9,128,128]{2,1,0:T(8,128)}, f32[9,32,128]{2,1,0:T(8,128)}), (f32[9,128,32]{1,2,0:T(8,128)}, f32[9,128,128]{2,1,0:T(8,128)}, f32[9,32,128]{2,1,0:T(8,128)})) %all-reduce.24.cloned.1.call-update) | async-done | bytes 884752 | tf_op jit(solution)/shard_map/psum | solution.py:227
  486.7 1.6 copy.283
  488.3 2.0 copy.284
  (299 shorter events, 83.0 us)
Async XLA Ops:
  7.2 479.6 %all-reduce.24.cloned.1.call-start = ((), (), s32[]{:S(2)}) async-start(), calls=%async_computation | async-start | bytes 1769472 | tf_op jit(solution)/shard_map/psum | solution.py:227
  8.5 10.9 %copy-start.18 = (s32[4,8,256]{2,1,0:T(8,128)S(1)}, s32[4,8,256]{2,1,0:T(8,128)}, u32[]{:S(2)}) copy-start(s32[4,8,256]{2,1,0:T(8,128)} %param.18) | copy-start | bytes 98308
  19.4 7.4 %copy-start.12 = (f32[4,8,256]{2,1,0:T(8,128)}, f32[4,8,256]{2,1,0:T(8,128)S(1)}, u32[]{:S(2)}) copy-start(f32[4,8,256]{2,1,0:T(8,128)S(1)} %multiply_convert_fusion.6) | copy-start | bytes 98308
  22.0 9.1 %copy-start.7 = (bf16[32,8,256]{2,1,0:T(8,128)(2,1)S(1)}, bf16[32,8,256]{2,1,0:T(8,128)(2,1)}, u32[]{:S(2)}) copy-start(bf16[32,8,256]{2,1,0:T(8,128)(2,1)} %param.12) | copy-start | bytes 393220
  27.7 7.3 %collective-permute-start = (f32[1,4,264]{2,1,0:T(4,128)S(1)}, f32[1,4,264]{2,1,0:T(4,128)S(1)}, u32[]{:S(2)}, u32[]{:S(2)}) collective-permute-start(f32[1,4,264]{2,1,0:T(4,128)S(1)} %get-tuple-element.260), channel_id=1, source_target_pairs={{0,16},{16,32},{32,48},{48,64},{64,80},{80,96},{96,112},{112,128},... | collective-permute-start | bytes 12680 | tf_op jit(solution)/shard_map/ppermute | solution.py:17
  30.3 4.7 collective-permute-start.1
  31.2 12.5 %copy-start.15 = (bf16[32,8,256]{2,1,0:T(8,128)(2,1)S(1)}, bf16[32,8,256]{2,1,0:T(8,128)(2,1)}, u32[]{:S(2)}) copy-start(bf16[32,8,256]{2,1,0:T(8,128)(2,1)} %param.13) | copy-start | bytes 393220
  31.2 14.6 %collective-permute-start.10 = (bf16[32,4,256]{2,1,0:T(4,128)(2,1)S(1)}, bf16[32,4,256]{2,1,0:T(4,128)(2,1)S(1)}, u32[]{:S(2)}, u32[]{:S(2)}) collective-permute-start(bf16[32,4,256]{2,1,0:T(4,128)(2,1)S(1)} %get-tuple-element.250), channel_id=1, source_target_pairs={{16,0},{32,16},{48,32},{64,48},{80,64},{96,80},{112,96},{128,112},... | collective-permute-start | bytes 196616 | tf_op jit(solution)/shard_map/ppermute | solution.py:20
  35.0 10.7 %collective-permute-start.9 = (bf16[32,4,256]{2,1,0:T(4,128)(2,1)S(1)}, bf16[32,4,256]{2,1,0:T(4,128)(2,1)S(1)}, u32[]{:S(2)}, u32[]{:S(2)}) collective-permute-start(bf16[32,4,256]{2,1,0:T(4,128)(2,1)S(1)} %get-tuple-element.249), channel_id=1, source_target_pairs={{0,16},{16,32},{32,48},{48,64},{64,80},{80,96},{96,112},{112,128},... | collective-permute-start | bytes 196616 | tf_op jit(solution)/shard_map/ppermute | solution.py:17
  35.1 8.3 %collective-permute-start.2 = (f32[1,24,4]{2,1,0:T(8,128)S(1)}, f32[1,24,4]{2,1,0:T(8,128)S(1)}, u32[]{:S(2)}, u32[]{:S(2)}) collective-permute-start(f32[1,24,4]{2,1,0:T(8,128)S(1)} %get-tuple-element.253), channel_id=1, source_target_pairs={{0,1},{1,2},{2,3},{3,4},{4,5},{5,6},{6,7},{7,8},{8,9},{9,10},{10,1... | collective-permute-start | bytes 1160 | tf_op jit(solution)/shard_map/ppermute | solution.py:17
  35.4 8.0 %collective-permute-start.3 = (f32[1,24,4]{2,1,0:T(8,128)S(1)}, f32[1,24,4]{2,1,0:T(8,128)S(1)}, u32[]{:S(2)}, u32[]{:S(2)}) collective-permute-start(f32[1,24,4]{2,1,0:T(8,128)S(1)} %get-tuple-element.254), channel_id=1, source_target_pairs={{1,0},{2,1},{3,2},{4,3},{5,4},{6,5},{7,6},{8,7},{9,8},{10,9},{11,1... | collective-permute-start | bytes 1160 | tf_op jit(solution)/shard_map/ppermute | solution.py:20
  44.3 7.3 %collective-permute-start.4 = (bf16[32,4,256]{2,1,0:T(4,128)(2,1)S(1)}, bf16[32,4,256]{2,1,0:T(4,128)(2,1)S(1)}, u32[]{:S(2)}, u32[]{:S(2)}) collective-permute-start(bf16[32,4,256]{2,1,0:T(4,128)(2,1)S(1)} %get-tuple-element.251), channel_id=1, source_target_pairs={{0,16},{16,32},{32,48},{48,64},{64,80},{80,96},{96,112},{112,128},... | collective-permute-start | bytes 196616 | tf_op jit(solution)/shard_map/ppermute | solution.py:17
  45.0 6.6 %collective-permute-start.5 = (bf16[32,4,256]{2,1,0:T(4,128)(2,1)S(1)}, bf16[32,4,256]{2,1,0:T(4,128)(2,1)S(1)}, u32[]{:S(2)}, u32[]{:S(2)}) collective-permute-start(bf16[32,4,256]{2,1,0:T(4,128)(2,1)S(1)} %get-tuple-element.252), channel_id=1, source_target_pairs={{16,0},{32,16},{48,32},{64,48},{80,64},{96,80},{112,96},{128,112},... | collective-permute-start | bytes 196616 | tf_op jit(solution)/shard_map/ppermute | solution.py:20
  46.0 24.8 %collective-permute-start.11 = (bf16[32,16,4]{2,1,0:T(8,128)(2,1)S(1)}, bf16[32,16,4]{2,1,0:T(8,128)(2,1)S(1)}, u32[]{:S(2)}, u32[]{:S(2)}) collective-permute-start(bf16[32,16,4]{2,1,0:T(8,128)(2,1)S(1)} %get-tuple-element.245), channel_id=1, source_target_pairs={{0,1},{1,2},{2,3},{3,4},{4,5},{5,6},{6,7},{7,8},{8,9},{9,10},{10,1... | collective-permute-start | bytes 12296 | tf_op jit(solution)/shard_map/ppermute | solution.py:17
  46.1 24.7 %collective-permute-start.12 = (bf16[32,16,4]{2,1,0:T(8,128)(2,1)S(1)}, bf16[32,16,4]{2,1,0:T(8,128)(2,1)S(1)}, u32[]{:S(2)}, u32[]{:S(2)}) collective-permute-start(bf16[32,16,4]{2,1,0:T(8,128)(2,1)S(1)} %get-tuple-element.246), channel_id=1, source_target_pairs={{1,0},{2,1},{3,2},{4,3},{5,4},{6,5},{7,6},{8,7},{9,8},{10,9},{11,1... | collective-permute-start | bytes 12296 | tf_op jit(solution)/shard_map/ppermute | solution.py:20
  51.9 18.9 %collective-permute-start.6 = (bf16[32,16,4]{2,1,0:T(8,128)(2,1)S(1)}, bf16[32,16,4]{2,1,0:T(8,128)(2,1)S(1)}, u32[]{:S(2)}, u32[]{:S(2)}) collective-permute-start(bf16[32,16,4]{2,1,0:T(8,128)(2,1)S(1)} %get-tuple-element.247), channel_id=1, source_target_pairs={{0,1},{1,2},{2,3},{3,4},{4,5},{5,6},{6,7},{7,8},{8,9},{9,10},{10,1... | collective-permute-start | bytes 12296 | tf_op jit(solution)/shard_map/ppermute | solution.py:17
  52.0 20.8 %collective-permute-start.7 = (bf16[32,16,4]{2,1,0:T(8,128)(2,1)S(1)}, bf16[32,16,4]{2,1,0:T(8,128)(2,1)S(1)}, u32[]{:S(2)}, u32[]{:S(2)}) collective-permute-start(bf16[32,16,4]{2,1,0:T(8,128)(2,1)S(1)} %get-tuple-element.248), channel_id=1, source_target_pairs={{1,0},{2,1},{3,2},{4,3},{5,4},{6,5},{7,6},{8,7},{9,8},{10,9},{11,1... | collective-permute-start | bytes 12296 | tf_op jit(solution)/shard_map/ppermute | solution.py:20
  74.5 5.3 %collective-permute-start.8 = (bf16[2,32,8,256]{3,2,1,0:T(8,128)(2,1)S(1)}, bf16[2,32,8,256]{3,2,1,0:T(8,128)(2,1)S(1)}, u32[]{:S(2)}, u32[]{:S(2)}) collective-permute-start(bf16[2,32,8,256]{3,2,1,0:T(8,128)(2,1)S(1)} %maximum_select_fusion.3), channel_id=1, source_target_pairs={{0,128},{16,144},{32,160},{48,176},{64,192},{80,208},{96,224},{112... | collective-permute-start | bytes 786440 | tf_op jit(solution)/shard_map/ppermute | solution.py:28
  75.8 6.8 %collective-permute-start.13 = (bf16[2,32,8,256]{3,2,1,0:T(8,128)(2,1)S(1)}, bf16[2,32,8,256]{3,2,1,0:T(8,128)(2,1)S(1)}, u32[]{:S(2)}, u32[]{:S(2)}) collective-permute-start(bf16[2,32,8,256]{3,2,1,0:T(8,128)(2,1)S(1)} %maximum_select_fusion.4), channel_id=1, source_target_pairs={{0,128},{16,144},{32,160},{48,176},{64,192},{80,208},{96,224},{112... | collective-permute-start | bytes 786440 | tf_op jit(solution)/shard_map/ppermute | solution.py:28
  99.7 1.0 copy-start.8
  100.9 4.2 copy-start.9
  115.4 1.2 copy-start.20
  137.1 4.2 copy-start.9
  151.7 1.2 copy-start.20
  156.7 9.6 %copy-start.1 = (f32[9,128,128]{2,1,0:T(8,128)}, f32[9,128,128]{2,1,0:T(8,128)S(1)}, u32[]{:S(2)}) copy-start(f32[9,128,128]{2,1,0:T(8,128)S(1)} %get-tuple-element.135) | copy-start | bytes 1769476
  156.7 9.6 %copy-start.3 = (f32[9,128,32]{1,2,0:T(8,128)}, f32[9,128,32]{1,2,0:T(8,128)S(1)}, u32[]{:S(2)}) copy-start(f32[9,128,32]{1,2,0:T(8,128)S(1)} %get-tuple-element.134) | copy-start | bytes 442372
  156.7 8.2 %collective-permute-start.14 = (f32[2,32,8,256]{3,2,1,0:T(8,128)}, f32[2,32,8,256]{3,2,1,0:T(8,128)S(1)}, u32[]{:S(2)}, u32[]{:S(2)}) collective-permute-start(f32[2,32,8,256]{3,2,1,0:T(8,128)} %get-tuple-element.133), channel_id=1, source_target_pairs={{0,128},{16,144},{32,160},{48,176},{64,192},{80,208},{96,224},{112... | collective-permute-start | bytes 1572872 | tf_op jit(solution)/shard_map/ppermute | solution.py:28
  199.6 11.8 %collective-permute-start.15 = (f32[32,4,264]{2,1,0:T(4,128)S(1)}, f32[32,4,264]{2,1,0:T(4,128)S(1)}, u32[]{:S(2)}, u32[]{:S(2)}) collective-permute-start(f32[32,4,264]{2,1,0:T(4,128)S(1)} %get-tuple-element.239), channel_id=1, source_target_pairs={{0,16},{16,32},{32,48},{48,64},{64,80},{80,96},{96,112},{112,128},... | collective-permute-start | bytes 405512 | tf_op jit(solution)/shard_map/ppermute | solution.py:17
  208.8 9.2 %collective-permute-start.16 = (f32[32,4,264]{2,1,0:T(4,128)S(1)}, f32[32,4,264]{2,1,0:T(4,128)S(1)}, u32[]{:S(2)}, u32[]{:S(2)}) collective-permute-start(f32[32,4,264]{2,1,0:T(4,128)S(1)} %get-tuple-element.240), channel_id=1, source_target_pairs={{16,0},{32,16},{48,32},{64,48},{80,64},{96,80},{112,96},{128,112},... | collective-permute-start | bytes 405512 | tf_op jit(solution)/shard_map/ppermute | solution.py:20
  218.3 16.7 %collective-permute-start.17 = (f32[32,24,4]{2,1,0:T(8,128)S(1)}, f32[32,24,4]{2,1,0:T(8,128)S(1)}, u32[]{:S(2)}, u32[]{:S(2)}) collective-permute-start(f32[32,24,4]{2,1,0:T(8,128)S(1)} %get-tuple-element.237), channel_id=1, source_target_pairs={{0,1},{1,2},{2,3},{3,4},{4,5},{5,6},{6,7},{7,8},{8,9},{9,10},{10,1... | collective-permute-start | bytes 36872 | tf_op jit(solution)/shard_map/ppermute | solution.py:17
  218.4 17.4 %collective-permute-start.18 = (f32[32,24,4]{2,1,0:T(8,128)S(1)}, f32[32,24,4]{2,1,0:T(8,128)S(1)}, u32[]{:S(2)}, u32[]{:S(2)}) collective-permute-start(f32[32,24,4]{2,1,0:T(8,128)S(1)} %get-tuple-element.238), channel_id=1, source_target_pairs={{1,0},{2,1},{3,2},{4,3},{5,4},{6,5},{7,6},{8,7},{9,8},{10,9},{11,1... | collective-permute-start | bytes 36872 | tf_op jit(solution)/shard_map/ppermute | solution.py:20
  488.3 2.0 copy-start.14
  (16 other events, 14.3 us)
Sparse Core Ops, SparseCore 0:
  218.5 268.2 all-reduce.23
where the time goes:
time: 507 us; the launch traced here: 498 us
  waiting for transfers between devices  279 us (55%)
  starting transfers between devices  63.2 us (12%)
  matrix products  60.3 us (12%)
  local copies, waits for them, and re-layouts  53.6 us (11%)
  between operations  30.9 us (6%)
  other arithmetic  10.7 us (2%)
    psum x1, waiting for transfers between devices, shards(): summed_grads = lax.psum((totals[0], totals[1], totals[2]), ('lat', 'lon'))  248 us
    ppermute x8, starting transfers between devices, extended_2(): lax.ppermute(lax.slice_in_dim(block, 0, width, axis=dim), axis, backward)  47.8 us
    dynamic_update_slice x8, local copies, waits for them, and re-layouts, place_slots(): lax.dynamic_update_slice(canvas, current + per_slot[slot_index], corner)  34.6 us
    dot_general x54, matrix products, kernel_grad(): jnp.einsum('ohw,khw->ok', cotangent, padded[:, tap_row:tap_row + height,...  25.4 us
    dot_general x54, matrix products, forward_conv(): jnp.einsum('ok,khw->ohw', kernel[tap_index], padded[:, tap_row:tap_row +...  21.3 us
    dot_general x36, matrix products, backward_conv(): jnp.einsum('ok,ohw->khw', kernel[tap_index], padded[:, 2 - tap_row:2 - ta...  13.6 us
    ppermute x8, starting transfers between devices, extended_2(): lax.ppermute(lax.slice_in_dim(block, block.shape[dim] - width, None, axis...  13 us
    ppermute x3, waiting for transfers between devices, shifted(): return lax.ppermute(value, axis, pairs)  12.8 us
  transfers between devices with their start and end apart: 20, of which 9 were waited for; matrix products, arithmetic and copies ran while one was open for 1% of the time, Pallas kernels for 0%

commit v1 on v0

--- a/solution.py
+++ b/solution.py
@@ -224,7 +224,7 @@
     weighted = weights[:, None] * outputs
     numerator = fold_canvas(place_slots(weighted), keep_top, keep_bottom)
     blended = numerator / total_weight
-    summed_grads = lax.psum((totals[0], totals[1], totals[2]), ("lat", "lon"))
+    summed_grads = lax.psum(lax.psum((totals[0], totals[1], totals[2]), "lat"), "lon")
     return (blended, summed_grads[0], summed_grads[1], summed_grads[2])
 
 

time: 507 us -> 474 us (0.935)
  the two profiles are of different devices: /device:TPU:1 before, /device:TPU:2 now
where the time goes in v1:
time: 474 us; the launch traced here: 465 us
  waiting for transfers between devices  253 us (53%)
  matrix products  60.3 us (13%)
  starting transfers between devices  57.4 us (12%)
  local copies, waits for them, and re-layouts  52.7 us (11%)
  between operations  31 us (7%)
  other arithmetic  9.5 us (2%)
    psum x1, waiting for transfers between devices, shards(): lax.psum(lax.psum((totals[0], totals[1], totals[2]), 'lat'), 'lon')  164 us
    psum x1, waiting for transfers between devices, shards(): lax.psum((totals[0], totals[1], totals[2]), 'lat')  50.6 us
    ppermute x8, starting transfers between devices, extended_2(): lax.ppermute(lax.slice_in_dim(block, 0, width, axis=dim), axis, backward)  45.3 us
    dynamic_update_slice x8, local copies, waits for them, and re-layouts, place_slots(): lax.dynamic_update_slice(canvas, current + per_slot[slot_index], corner)  34.3 us
    dot_general x54, matrix products, kernel_grad(): jnp.einsum('ohw,khw->ok', cotangent, padded[:, tap_row:tap_row + height,...  25.4 us
    dot_general x54, matrix products, forward_conv(): jnp.einsum('ok,khw->ohw', kernel[tap_index], padded[:, tap_row:tap_row +...  21.3 us
    ppermute x3, waiting for transfers between devices, shifted(): return lax.ppermute(value, axis, pairs)  18.2 us
    dot_general x36, matrix products, backward_conv(): jnp.einsum('ok,ohw->khw', kernel[tap_index], padded[:, 2 - tap_row:2 - ta...  13.6 us
  transfers between devices with their start and end apart: 21, of which 11 were waited for; matrix products, arithmetic and copies ran while one was open for 8% of the time, Pallas kernels for 0%

profile of v1, /device:TPU:2, one launch (start us, length us, event | category | flops | bytes accessed | tf_op | source)
XLA Modules:
  0.0 464.7 jit_solution(8719502334967729556)
XLA Ops:
  28.1 1.6 collective-permute-start.1
  31.0 1.9 collective-permute-start.2
  33.0 7.0 %collective-permute-start.3 = (f32[1,24,4]{2,1,0:T(8,128)S(1)}, f32[1,24,4]{2,1,0:T(8,128)S(1)}, u32[]{:S(2)}, u32[]{:S(2)}) collective-permute-start(f32[1,24,4]{2,1,0:T(8,128)S(1)} %get-tuple-element.257), channel_id=1, source_target_pairs={{1,0},{2,1},{3,2},{4,3},{5,4},{6,5},{7,6},{8,7},{9,8},{10,9},{11,1... | collective-permute-start | bytes 1160 | tf_op jit(solution)/shard_map/ppermute | solution.py:20
  40.0 1.6 collective-permute-done.2
  42.7 1.6 collective-permute-start.5
  44.7 5.9 %collective-permute-start.12 = (bf16[32,16,4]{2,1,0:T(8,128)(2,1)S(1)}, bf16[32,16,4]{2,1,0:T(8,128)(2,1)S(1)}, u32[]{:S(2)}, u32[]{:S(2)}) collective-permute-start(bf16[32,16,4]{2,1,0:T(8,128)(2,1)S(1)} %get-tuple-element.249), channel_id=1, source_target_pairs={{1,0},{2,1},{3,2},{4,3},{5,4},{6,5},{7,6},{8,7},{9,8},{10,9},{11,1... | collective-permute-start | bytes 12296 | tf_op jit(solution)/shard_map/ppermute | solution.py:20
  50.9 19.4 %collective-permute-start.7 = (bf16[32,16,4]{2,1,0:T(8,128)(2,1)S(1)}, bf16[32,16,4]{2,1,0:T(8,128)(2,1)S(1)}, u32[]{:S(2)}, u32[]{:S(2)}) collective-permute-start(bf16[32,16,4]{2,1,0:T(8,128)(2,1)S(1)} %get-tuple-element.251), channel_id=1, source_target_pairs={{1,0},{2,1},{3,2},{4,3},{5,4},{6,5},{7,6},{8,7},{9,8},{10,9},{11,1... | collective-permute-start | bytes 12296 | tf_op jit(solution)/shard_map/ppermute | solution.py:20
  70.3 2.5 collective-permute-done.7
  72.8 1.0 maximum_select_fusion.2
  75.6 1.7 collective-permute-start.13
  77.4 6.1 %collective-permute-done.8 = bf16[2,32,8,256]{3,2,1,0:T(8,128)(2,1)S(1)} collective-permute-done((bf16[2,32,8,256]{3,2,1,0:T(8,128)(2,1)S(1)}, bf16[2,32,8,256]{3,2,1,0:T(8,128)(2,1)S(1)}, u32[]{:S(2)}, u32[]{:S(2)}) %collective-permute-start.8) | collective-permute-done | bytes 262176 | tf_op jit(solution)/shard_map/ppermute | solution.py:28
  84.0 2.2 collective-permute-done.13
  87.8 72.5 %while.19 = (s32[]{:T(128)}, f32[9,128,32]{1,2,0:T(8,128)S(1)}, f32[9,128,128]{2,1,0:T(8,128)S(1)}, f32[9,32,128]{2,1,0:T(8,128)}, f32[2,32,8,256]{3,2,1,0:T(8,1...) while((s32[]{:T(128)}, f32[9,128,32]{1,2,0:T(8,128)S(1)}, ...), condition=%wide.region_1.3_spmd.clone, body=%wide.region_0.2_spmd.clone.sunk | while | flops 2583609344 | bytes 133587216 | solution.py:110
  92.3 1.5 multiply_convert_fusion.8
  112.1 1.6 select_add_fusion.8
  128.5 1.5 multiply_convert_fusion.8
  148.3 1.7 select_add_fusion.8
  160.4 1.4 collective-permute-start.14
  161.9 9.9 %collective-permute-done.14 = f32[2,32,8,256]{3,2,1,0:T(8,128)S(1)} collective-permute-done((f32[2,32,8,256]{3,2,1,0:T(8,128)}, f32[2,32,8,256]{3,2,1,0:T(8,128)S(1)}, u32[]{:S(2)}, u32[]{:S(2)}) %collective-permute-start.14) | collective-permute-done | bytes 524320 | tf_op jit(solution)/shard_map/ppermute | solution.py:28
  173.0 1.3 dynamic_update_slice.35
  174.4 10.0 %dynamic_update_slice.36 = f32[32,16,264]{2,1,0:T(8,128)S(1)} dynamic-update-slice(f32[32,16,264]{2,1,0:T(8,128)S(1)} %dynamic_update_slice.35, f32[32,8,256]{2,1,0:T(8,128)S(1)} %fusion.200, s32[]{:T(128)} %constant.84.clone.1, s32[]{:T(128)S(6)} %select_n.138, s32[]{:T(128)S(6)} %select_n.139) | dynamic-update-slice | bytes 524292 | tf_op jit(solution)/shard_map/dynamic_update_slice | solution.py:162
  184.6 10.1 %dynamic_update_slice.37 = f32[32,16,264]{2,1,0:T(8,128)S(1)} dynamic-update-slice(f32[32,16,264]{2,1,0:T(8,128)S(1)} %dynamic_update_slice.36, f32[32,8,256]{2,1,0:T(8,128)S(1)} %fusion.199, s32[]{:T(128)} %constant.84.clone.1, s32[]{:T(128)S(6)} %select_n.140, s32[]{:T(128)S(6)} %select_n.141) | dynamic-update-slice | bytes 524292 | tf_op jit(solution)/shard_map/dynamic_update_slice | solution.py:162
  194.9 10.2 %dynamic_update_slice.38 = f32[32,16,264]{2,1,0:T(8,128)S(1)} dynamic-update-slice(f32[32,16,264]{2,1,0:T(8,128)S(1)} %dynamic_update_slice.37, f32[32,8,256]{2,1,0:T(8,128)S(1)} %fusion.198, s32[]{:T(128)} %constant.84.clone.1, s32[]{:T(128)S(6)} %select_n.142, s32[]{:T(128)S(6)} %select_n.143) | dynamic-update-slice | bytes 524292 | tf_op jit(solution)/shard_map/dynamic_update_slice | solution.py:162
  205.1 5.7 %collective-permute-start.15 = (f32[32,4,264]{2,1,0:T(4,128)S(1)}, f32[32,4,264]{2,1,0:T(4,128)S(1)}, u32[]{:S(2)}, u32[]{:S(2)}) collective-permute-start(f32[32,4,264]{2,1,0:T(4,128)S(1)} %get-tuple-element.242), channel_id=1, source_target_pairs={{0,16},{16,32},{32,48},{48,64},{64,80},{80,96},{96,112},{112,128},... | collective-permute-start | bytes 405512 | tf_op jit(solution)/shard_map/ppermute | solution.py:17
  210.8 1.1 collective-permute-done.15
  211.9 4.9 %collective-permute-done.16 = f32[32,4,264]{2,1,0:T(4,128)S(1)} collective-permute-done((f32[32,4,264]{2,1,0:T(4,128)S(1)}, f32[32,4,264]{2,1,0:T(4,128)S(1)}, u32[]{:S(2)}, u32[]{:S(2)}) %collective-permute-start.16) | collective-permute-done | bytes 135200 | tf_op jit(solution)/shard_map/ppermute | solution.py:20
  217.1 9.0 %collective-permute-start.18 = (f32[32,24,4]{2,1,0:T(8,128)S(1)}, f32[32,24,4]{2,1,0:T(8,128)S(1)}, u32[]{:S(2)}, u32[]{:S(2)}) collective-permute-start(f32[32,24,4]{2,1,0:T(8,128)S(1)} %get-tuple-element.241), channel_id=1, source_target_pairs={{1,0},{2,1},{3,2},{4,3},{5,4},{6,5},{7,6},{8,7},{9,8},{10,9},{11,1... | collective-permute-start | bytes 36872 | tf_op jit(solution)/shard_map/ppermute | solution.py:20
  226.1 9.6 %collective-permute-done.17 = f32[32,24,4]{2,1,0:T(8,128)S(1)} collective-permute-done((f32[32,24,4]{2,1,0:T(8,128)S(1)}, f32[32,24,4]{2,1,0:T(8,128)S(1)}, u32[]{:S(2)}, u32[]{:S(2)}) %collective-permute-start.17) | collective-permute-done | bytes 12320 | tf_op jit(solution)/shard_map/ppermute | solution.py:17
  236.5 50.6 %all-reduce.28.cloned.1.call-done = (f32[9,128,32]{1,2,0:T(8,128)}, f32[9,128,128]{2,1,0:T(8,128)}, f32[9,32,128]{2,1,0:T(8,128)}) async-done(((f32[9,128,32]{1,2,0:T(8,128)}, f32[9,128,128]{2,1,0:T(8,128)}, f32[9,32,128]{2,1,0:T(8,128)}), (f32[9,128,32]{1,2,0:T(8,128)}, f32[9,128,128]{2,1,0:T(8,128)}, f32[9,32,128]{2,1,0:T(8,128)})) %all-reduce.28.cloned.1.call-update) | async-done | bytes 884752 | tf_op jit(solution)/shard_map/psum | solution.py:227
  289.2 164.1 %all-reduce.26.cloned.1.call-done = (f32[9,128,32]{1,2,0:T(8,128)}, f32[9,128,128]{2,1,0:T(8,128)}, f32[9,32,128]{2,1,0:T(8,128)}) async-done(((f32[9,128,32]{1,2,0:T(8,128)}, f32[9,128,128]{2,1,0:T(8,128)}, f32[9,32,128]{2,1,0:T(8,128)}), (f32[9,128,32]{1,2,0:T(8,128)}, f32[9,128,128]{2,1,0:T(8,128)}, f32[9,32,128]{2,1,0:T(8,128)})) %all-reduce.26.cloned.1.call-update) | async-done | bytes 884752 | tf_op jit(solution)/shard_map/psum | solution.py:227
  453.3 1.6 copy.286
  454.9 2.0 copy.287
  (304 shorter events, 82.7 us)
Async XLA Ops:
  7.2 279.9 %all-reduce.28.cloned.1.call-start = ((), (), s32[]{:S(2)}) async-start(), calls=%async_computation.1 | async-start | bytes 1769472 | tf_op jit(solution)/shard_map/psum | solution.py:227
  8.5 10.9 %copy-start.19 = (s32[4,8,256]{2,1,0:T(8,128)S(1)}, s32[4,8,256]{2,1,0:T(8,128)}, u32[]{:S(2)}) copy-start(s32[4,8,256]{2,1,0:T(8,128)} %param.18) | copy-start | bytes 98308
  19.6 7.4 %copy-start.13 = (f32[4,8,256]{2,1,0:T(8,128)}, f32[4,8,256]{2,1,0:T(8,128)S(1)}, u32[]{:S(2)}) copy-start(f32[4,8,256]{2,1,0:T(8,128)S(1)} %multiply_convert_fusion.6) | copy-start | bytes 98308
  22.2 7.4 %copy-start.7 = (bf16[32,8,256]{2,1,0:T(8,128)(2,1)S(1)}, bf16[32,8,256]{2,1,0:T(8,128)(2,1)}, u32[]{:S(2)}) copy-start(bf16[32,8,256]{2,1,0:T(8,128)(2,1)} %param.12) | copy-start | bytes 393220
  27.8 3.1 collective-permute-start
  28.1 2.9 collective-permute-start.1
  29.7 12.2 %copy-start.16 = (bf16[32,8,256]{2,1,0:T(8,128)(2,1)S(1)}, bf16[32,8,256]{2,1,0:T(8,128)(2,1)}, u32[]{:S(2)}) copy-start(bf16[32,8,256]{2,1,0:T(8,128)(2,1)} %param.13) | copy-start | bytes 393220
  29.7 14.6 %collective-permute-start.10 = (bf16[32,4,256]{2,1,0:T(4,128)(2,1)S(1)}, bf16[32,4,256]{2,1,0:T(4,128)(2,1)S(1)}, u32[]{:S(2)}, u32[]{:S(2)}) collective-permute-start(bf16[32,4,256]{2,1,0:T(4,128)(2,1)S(1)} %get-tuple-element.253), channel_id=1, source_target_pairs={{16,0},{32,16},{48,32},{64,48},{80,64},{96,80},{112,96},{128,112},... | collective-permute-start | bytes 196616 | tf_op jit(solution)/shard_map/ppermute | solution.py:20
  30.6 13.8 %collective-permute-start.9 = (bf16[32,4,256]{2,1,0:T(4,128)(2,1)S(1)}, bf16[32,4,256]{2,1,0:T(4,128)(2,1)S(1)}, u32[]{:S(2)}, u32[]{:S(2)}) collective-permute-start(bf16[32,4,256]{2,1,0:T(4,128)(2,1)S(1)} %get-tuple-element.252), channel_id=1, source_target_pairs={{0,16},{16,32},{32,48},{48,64},{64,80},{80,96},{96,112},{112,128},... | collective-permute-start | bytes 196616 | tf_op jit(solution)/shard_map/ppermute | solution.py:17
  31.0 10.5 %collective-permute-start.2 = (f32[1,24,4]{2,1,0:T(8,128)S(1)}, f32[1,24,4]{2,1,0:T(8,128)S(1)}, u32[]{:S(2)}, u32[]{:S(2)}) collective-permute-start(f32[1,24,4]{2,1,0:T(8,128)S(1)} %get-tuple-element.256), channel_id=1, source_target_pairs={{0,1},{1,2},{2,3},{3,4},{4,5},{5,6},{6,7},{7,8},{8,9},{9,10},{10,1... | collective-permute-start | bytes 1160 | tf_op jit(solution)/shard_map/ppermute | solution.py:17
  33.0 8.6 %collective-permute-start.3 = (f32[1,24,4]{2,1,0:T(8,128)S(1)}, f32[1,24,4]{2,1,0:T(8,128)S(1)}, u32[]{:S(2)}, u32[]{:S(2)}) collective-permute-start(f32[1,24,4]{2,1,0:T(8,128)S(1)} %get-tuple-element.257), channel_id=1, source_target_pairs={{1,0},{2,1},{3,2},{4,3},{5,4},{6,5},{7,6},{8,7},{9,8},{10,9},{11,1... | collective-permute-start | bytes 1160 | tf_op jit(solution)/shard_map/ppermute | solution.py:20
  42.5 8.1 %collective-permute-start.4 = (bf16[32,4,256]{2,1,0:T(4,128)(2,1)S(1)}, bf16[32,4,256]{2,1,0:T(4,128)(2,1)S(1)}, u32[]{:S(2)}, u32[]{:S(2)}) collective-permute-start(bf16[32,4,256]{2,1,0:T(4,128)(2,1)S(1)} %get-tuple-element.254), channel_id=1, source_target_pairs={{0,16},{16,32},{32,48},{48,64},{64,80},{80,96},{96,112},{112,128},... | collective-permute-start | bytes 196616 | tf_op jit(solution)/shard_map/ppermute | solution.py:17
  42.7 7.9 %collective-permute-start.5 = (bf16[32,4,256]{2,1,0:T(4,128)(2,1)S(1)}, bf16[32,4,256]{2,1,0:T(4,128)(2,1)S(1)}, u32[]{:S(2)}, u32[]{:S(2)}) collective-permute-start(bf16[32,4,256]{2,1,0:T(4,128)(2,1)S(1)} %get-tuple-element.255), channel_id=1, source_target_pairs={{16,0},{32,16},{48,32},{64,48},{80,64},{96,80},{112,96},{128,112},... | collective-permute-start | bytes 196616 | tf_op jit(solution)/shard_map/ppermute | solution.py:20
  44.6 25.7 %collective-permute-start.11 = (bf16[32,16,4]{2,1,0:T(8,128)(2,1)S(1)}, bf16[32,16,4]{2,1,0:T(8,128)(2,1)S(1)}, u32[]{:S(2)}, u32[]{:S(2)}) collective-permute-start(bf16[32,16,4]{2,1,0:T(8,128)(2,1)S(1)} %get-tuple-element.248), channel_id=1, source_target_pairs={{0,1},{1,2},{2,3},{3,4},{4,5},{5,6},{6,7},{7,8},{8,9},{9,10},{10,1... | collective-permute-start | bytes 12296 | tf_op jit(solution)/shard_map/ppermute | solution.py:17
  44.7 25.6 %collective-permute-start.12 = (bf16[32,16,4]{2,1,0:T(8,128)(2,1)S(1)}, bf16[32,16,4]{2,1,0:T(8,128)(2,1)S(1)}, u32[]{:S(2)}, u32[]{:S(2)}) collective-permute-start(bf16[32,16,4]{2,1,0:T(8,128)(2,1)S(1)} %get-tuple-element.249), channel_id=1, source_target_pairs={{1,0},{2,1},{3,2},{4,3},{5,4},{6,5},{7,6},{8,7},{9,8},{10,9},{11,1... | collective-permute-start | bytes 12296 | tf_op jit(solution)/shard_map/ppermute | solution.py:20
  50.8 19.5 %collective-permute-start.6 = (bf16[32,16,4]{2,1,0:T(8,128)(2,1)S(1)}, bf16[32,16,4]{2,1,0:T(8,128)(2,1)S(1)}, u32[]{:S(2)}, u32[]{:S(2)}) collective-permute-start(bf16[32,16,4]{2,1,0:T(8,128)(2,1)S(1)} %get-tuple-element.250), channel_id=1, source_target_pairs={{0,1},{1,2},{2,3},{3,4},{4,5},{5,6},{6,7},{7,8},{8,9},{9,10},{10,1... | collective-permute-start | bytes 12296 | tf_op jit(solution)/shard_map/ppermute | solution.py:17
  50.9 21.9 %collective-permute-start.7 = (bf16[32,16,4]{2,1,0:T(8,128)(2,1)S(1)}, bf16[32,16,4]{2,1,0:T(8,128)(2,1)S(1)}, u32[]{:S(2)}, u32[]{:S(2)}) collective-permute-start(bf16[32,16,4]{2,1,0:T(8,128)(2,1)S(1)} %get-tuple-element.251), channel_id=1, source_target_pairs={{1,0},{2,1},{3,2},{4,3},{5,4},{6,5},{7,6},{8,7},{9,8},{10,9},{11,1... | collective-permute-start | bytes 12296 | tf_op jit(solution)/shard_map/ppermute | solution.py:20
  74.6 8.8 %collective-permute-start.8 = (bf16[2,32,8,256]{3,2,1,0:T(8,128)(2,1)S(1)}, bf16[2,32,8,256]{3,2,1,0:T(8,128)(2,1)S(1)}, u32[]{:S(2)}, u32[]{:S(2)}) collective-permute-start(bf16[2,32,8,256]{3,2,1,0:T(8,128)(2,1)S(1)} %maximum_select_fusion.3), channel_id=1, source_target_pairs={{0,128},{16,144},{32,160},{48,176},{64,192},{80,208},{96,224},{112... | collective-permute-start | bytes 786440 | tf_op jit(solution)/shard_map/ppermute | solution.py:28
  75.6 10.6 %collective-permute-start.13 = (bf16[2,32,8,256]{3,2,1,0:T(8,128)(2,1)S(1)}, bf16[2,32,8,256]{3,2,1,0:T(8,128)(2,1)S(1)}, u32[]{:S(2)}, u32[]{:S(2)}) collective-permute-start(bf16[2,32,8,256]{3,2,1,0:T(8,128)(2,1)S(1)} %maximum_select_fusion.4), channel_id=1, source_target_pairs={{0,128},{16,144},{32,160},{48,176},{64,192},{80,208},{96,224},{112... | collective-permute-start | bytes 786440 | tf_op jit(solution)/shard_map/ppermute | solution.py:28
  104.5 4.2 copy-start.9
  140.7 4.2 copy-start.9
  160.3 1.5 copy-start.1
  160.4 1.5 copy-start.3
  160.4 11.5 %copy-start.10 = (f32[2,32,8,256]{3,2,1,0:T(8,128)S(1)}, f32[2,32,8,256]{3,2,1,0:T(8,128)}, u32[]{:S(2)}) copy-start(f32[2,32,8,256]{3,2,1,0:T(8,128)} %get-tuple-element.133) | copy-start | bytes 1572868
  160.4 11.5 %collective-permute-start.14 = (f32[2,32,8,256]{3,2,1,0:T(8,128)}, f32[2,32,8,256]{3,2,1,0:T(8,128)S(1)}, u32[]{:S(2)}, u32[]{:S(2)}) collective-permute-start(f32[2,32,8,256]{3,2,1,0:T(8,128)} %get-tuple-element.133), channel_id=1, source_target_pairs={{0,128},{16,144},{32,160},{48,176},{64,192},{80,208},{96,224},{112... | collective-permute-start | bytes 1572872 | tf_op jit(solution)/shard_map/ppermute | solution.py:28
  161.9 291.4 %all-reduce.26.cloned.1.call-start = ((), (), s32[]{:S(2)}) async-start(), calls=%async_computation | async-start | bytes 1769472 | tf_op jit(solution)/shard_map/psum | solution.py:227
  205.1 6.7 %collective-permute-start.15 = (f32[32,4,264]{2,1,0:T(4,128)S(1)}, f32[32,4,264]{2,1,0:T(4,128)S(1)}, u32[]{:S(2)}, u32[]{:S(2)}) collective-permute-start(f32[32,4,264]{2,1,0:T(4,128)S(1)} %get-tuple-element.242), channel_id=1, source_target_pairs={{0,16},{16,32},{32,48},{48,64},{64,80},{80,96},{96,112},{112,128},... | collective-permute-start | bytes 405512 | tf_op jit(solution)/shard_map/ppermute | solution.py:17
  210.8 6.0 %collective-permute-start.16 = (f32[32,4,264]{2,1,0:T(4,128)S(1)}, f32[32,4,264]{2,1,0:T(4,128)S(1)}, u32[]{:S(2)}, u32[]{:S(2)}) collective-permute-start(f32[32,4,264]{2,1,0:T(4,128)S(1)} %get-tuple-element.243), channel_id=1, source_target_pairs={{16,0},{32,16},{48,32},{64,48},{80,64},{96,80},{112,96},{128,112},... | collective-permute-start | bytes 405512 | tf_op jit(solution)/shard_map/ppermute | solution.py:20
  217.0 18.7 %collective-permute-start.17 = (f32[32,24,4]{2,1,0:T(8,128)S(1)}, f32[32,24,4]{2,1,0:T(8,128)S(1)}, u32[]{:S(2)}, u32[]{:S(2)}) collective-permute-start(f32[32,24,4]{2,1,0:T(8,128)S(1)} %get-tuple-element.240), channel_id=1, source_target_pairs={{0,1},{1,2},{2,3},{3,4},{4,5},{5,6},{6,7},{7,8},{8,9},{9,10},{10,1... | collective-permute-start | bytes 36872 | tf_op jit(solution)/shard_map/ppermute | solution.py:17
  217.1 18.6 %collective-permute-start.18 = (f32[32,24,4]{2,1,0:T(8,128)S(1)}, f32[32,24,4]{2,1,0:T(8,128)S(1)}, u32[]{:S(2)}, u32[]{:S(2)}) collective-permute-start(f32[32,24,4]{2,1,0:T(8,128)S(1)} %get-tuple-element.241), channel_id=1, source_target_pairs={{1,0},{2,1},{3,2},{4,3},{5,4},{6,5},{7,6},{8,7},{9,8},{10,9},{11,1... | collective-permute-start | bytes 36872 | tf_op jit(solution)/shard_map/ppermute | solution.py:20
  235.7 51.4 %copy-start.12 = (f32[32,24,4]{2,1,0:T(8,128)}, f32[32,24,4]{2,1,0:T(8,128)S(1)}, u32[]{:S(2)}) copy-start(f32[32,24,4]{2,1,0:T(8,128)S(1)} %collective-permute-done.18) | copy-start | bytes 36868
  454.9 2.0 copy-start.15
  (18 other events, 17.0 us)
Sparse Core Ops, SparseCore 0:
  162.0 125.0 all-reduce.27
  289.9 163.3 all-reduce.25
